TPU v7x, 256 devices: a whole 4x4x8 slice. The times are simulated.
256 devices in a mesh: row: 16 (over x, y_hi, core), col: 16 (over z, y_lo).
Axes of the slice: x: 4, y: 4 (y_hi: 2, y_lo: 2; y = y_hi * 2 + y_lo), z: 8, core: 2. Of those that a mesh axis runs over, the one named last changes fastest.
Arguments:
- panel_cols: bfloat16 [48, 4096, 512], P('col', 'row'), may hold values from -6 to 6
- inverses: bfloat16 [2, 256, 256], replicated, as said below
- trailing: bfloat16 [48, 4096, 4096], P(None, 'row', 'col'), may hold values from -6 to 6
Outputs:
- updated: bfloat16 [48, 4096, 4096], P(None, 'row', 'col')
Inputs may be any that keep to these rules, and one draw needn't show every extreme that they name: `inverses`: each of the two 256 x 256 matrices is lower triangular with a positive diagonal.
All inputs are finite; a program needn't handle non-finite values.
Results may differ from a plain program's by a relative error of at most 0.0063.
Values may be sent and summed in bfloat16 or wider, within the bound.
A program may use at most 128 MiB of HBM per device.

v0:
```python
import jax
import jax.numpy as jnp
from jax import lax
from jax.sharding import PartitionSpec as P


def broadcast(value, axis, source):
    kept = jnp.where(lax.axis_index(axis) == source, value, 0).astype(value.dtype)
    return lax.psum(kept, axis)


def shards(panel_cols, inverses, trailing):
    tile_size = panel_cols.shape[1]
    grid_rows = lax.axis_size("row")
    grid_cols = lax.axis_size("col")
    col_index = lax.axis_index("col")
    left_factor = jnp.einsum(
        "tak,bk->tab", panel_cols[:, :, :tile_size], inverses[0], preferred_element_type=jnp.float32
    ).astype(jnp.bfloat16)
    couple_tile = broadcast(left_factor[0], ("row", "col"), grid_cols)
    reduced = (
        panel_cols[:, :, tile_size:].astype(jnp.float32)
        - jnp.einsum("tak,bk->tab", left_factor, couple_tile, preferred_element_type=jnp.float32)
    ).astype(jnp.bfloat16)
    right_factor = jnp.einsum(
        "tak,bk->tab", reduced, inverses[1], preferred_element_type=jnp.float32
    ).astype(jnp.bfloat16)
    factored = jnp.concatenate([left_factor, right_factor], axis=2)
    root_row = (col_index + 2) % grid_rows
    source_tile = (col_index + 2) // grid_rows
    whole_panel = lax.all_gather(factored, "col", axis=0, tiled=True)
    key_tile = broadcast(
        lax.dynamic_index_in_dim(whole_panel, source_tile, 0, keepdims=False), "row", root_row
    )
    update_sum = jnp.einsum(
        "tak,bk->tab", whole_panel, key_tile, preferred_element_type=jnp.float32
    )
    return (trailing.astype(jnp.float32) - update_sum).astype(jnp.bfloat16)


def solution(mesh):
    in_specs = (P("col", "row", None), P(), P(None, "row", "col"))
    out_specs = P(None, "row", "col")
    return jax.shard_map(shards, mesh=mesh, in_specs=in_specs, out_specs=out_specs, check_vma=False)
```

profile of v0, /device:TPU:1, one launch (start us, length us, event | category | flops | bytes accessed | tf_op | source)
XLA Modules:
  0.0 691.7 jit_solution(11645885408623004183)
XLA Ops:
  6.5 0.0 all-reduce.3.cloned.1.call-start
  6.5 1.3 convolution_convert_fusion.1
  7.9 0.7 fusion.5
  8.5 0.0 all-reduce.3.cloned.1.call-update
  8.6 0.0 all-gather.2.cloned.1.call-start
  8.6 248.9 %all-reduce.3.cloned.1.call-done = bf16[256,256]{0,1:T(8,128)(2,1)} async-done(((bf16[256,256]{0,1:T(8,128)(2,1)}), bf16[256,256]{0,1:T(8,128)(2,1)}) %all-reduce.3.cloned.1.call-update) | async-done | bytes 131088 | tf_op jit(solution)/shard_map/psum | solution.py:9
  257.6 1.7 convolution_convert_fusion
  259.3 0.1 pad_maximum_fusion
  259.3 1.2 copy.6
  260.5 0.0 all-gather.2.cloned.1.call-update
  260.5 0.0 all-reduce.5.cloned.1.call-start
  260.6 264.4 %all-gather.2.cloned.1.call-done = bf16[48,256,512]{2,1,0:T(8,128)(2,1)} async-done(((bf16[3,256,512]{2,1,0:T(8,128)(2,1)}), bf16[48,256,512]{2,1,0:T(8,128)(2,1)}) %all-gather.2.cloned.1.call-update) | async-done | bytes 12582928 | tf_op jit(solution)/shard_map/all_gather | solution.py:31
  525.0 1.7 select_bitcast_fusion
  526.7 0.0 all-reduce.5.cloned.1.call-update
  526.7 145.8 %all-reduce.5.cloned.1.call-done = bf16[256,512]{1,0:T(8,128)(2,1)} async-done(((bf16[256,512]{1,0:T(8,128)(2,1)}), bf16[256,512]{1,0:T(8,128)(2,1)}) %all-reduce.5.cloned.1.call-update) | async-done | bytes 262160 | tf_op jit(solution)/shard_map/psum | solution.py:9
  672.5 12.6 %subtract_convert_fusion = bf16[48,256,256]{2,1,0:T(8,128)(2,1)} fusion(bf16[48,256,256]{2,1,0:T(8,128)(2,1)} %param.5, bf16[48,256,512]{2,1,0:T(8,128)(2,1)} %all-gather.2.cloned.1.call-done, bf16[256,512]{1,0:T(8,128)(2,1)} %all-reduce.5.cloned.1.call-done), kind=kOutput, calls=%fused_computation | convolution fusion | flops 3230662656 | bytes 25427968 | tf_op jit(solution)/shard_map/tak,bk->tab/dot_general | solution.py:35
Async XLA Ops:
  6.5 251.0 %all-reduce.3.cloned.1.call-start = ((), (), s32[]{:S(2)}) async-start(), calls=%async_computation | async-start | bytes 262144 | tf_op jit(solution)/shard_map/psum | solution.py:9
  8.6 516.4 %all-gather.2.cloned.1.call-start = ((), (), s32[]{:S(2)}) async-start(), calls=%async_computation.1 | async-start | bytes 13369344 | tf_op jit(solution)/shard_map/all_gather | solution.py:31
  260.5 412.0 %all-reduce.5.cloned.1.call-start = ((), (), s32[]{:S(2)}) async-start(), calls=%async_computation.2 | async-start | bytes 524288 | tf_op jit(solution)/shard_map/psum | solution.py:9
Sparse Core Ops, SparseCore 0:
  12.9 244.6 all-reduce.2
  260.6 264.3 all-gather.1
  527.6 144.8 all-reduce.4
where the time goes:
time: 692 us
  waiting for transfers between devices  659 us (95%)
  matrix products  15.7 us (2%)
  between operations  13.2 us (2%)
    psum x2, waiting for transfers between devices, broadcast(): return lax.psum(kept, axis)  395 us
    all_gather x1, waiting for transfers between devices, shards(): whole_panel = lax.all_gather(factored, 'col', axis=0, tiled=True)  264 us
  transfers between devices with their start and end apart: 3, of which 3 were waited for; matrix products, arithmetic and copies ran while one was open for 0% of the time, Pallas kernels for 0%

commit v1 on v0

--- a/solution.py
+++ b/solution.py
@@ -28,7 +28,9 @@
     factored = jnp.concatenate([left_factor, right_factor], axis=2)
     root_row = (col_index + 2) % grid_rows
     source_tile = (col_index + 2) // grid_rows
-    whole_panel = lax.all_gather(factored, "col", axis=0, tiled=True)
+    whole_panel = jnp.concatenate(
+        lax.all_to_all(jnp.stack([factored] * lax.axis_size("col")), "col", 0, 0), axis=0
+    )
     key_tile = broadcast(
         lax.dynamic_index_in_dim(whole_panel, source_tile, 0, keepdims=False), "row", root_row
     )

time: 692 us -> 724 us (1.046)
  waiting for transfers between devices: 659 us -> 680 us
    all_to_all x0 -> x1, waiting for transfers between devices: none -> 284 us  [shards(): lax.all_to_all(jnp.stack([factored] * lax.axis_size('col')), 'col', 0, 0)]
    all_gather x1 -> x0, waiting for transfers between devices: 264 us -> none  [shards(): whole_panel = lax.all_gather(factored, 'col', axis=0, tiled=True)]
where the time goes in v1:
time: 724 us
  waiting for transfers between devices  680 us (94%)
  matrix products  15.6 us (2%)
  between operations  13.5 us (2%)
    psum x2, waiting for transfers between devices, broadcast(): return lax.psum(kept, axis)  397 us
    all_to_all x1, waiting for transfers between devices, shards(): lax.all_to_all(jnp.stack([factored] * lax.axis_size('col')), 'col', 0, 0)  284 us
  transfers between devices with their start and end apart: 3, of which 3 were waited for; matrix products, arithmetic and copies ran while one was open for 0% of the time, Pallas kernels for 0%

profile of v1, /device:TPU:1, one launch (start us, length us, event | category | flops | bytes accessed | tf_op | source)
XLA Modules:
  0.0 723.6 jit_solution(6813487442443535291)
XLA Ops:
  6.5 0.0 all-reduce.3.cloned.1.call-start
  6.5 1.3 convolution_convert_fusion.1
  7.9 0.7 fusion.5
  8.5 0.0 all-reduce.3.cloned.1.call-update
  8.6 249.0 %all-reduce.3.cloned.1.call-done = bf16[256,256]{0,1:T(8,128)(2,1)} async-done(((bf16[256,256]{0,1:T(8,128)(2,1)}), bf16[256,256]{0,1:T(8,128)(2,1)}) %all-reduce.3.cloned.1.call-update) | async-done | bytes 131088 | tf_op jit(solution)/shard_map/psum | solution.py:9
  257.6 1.7 convolution_convert_fusion
  259.3 0.1 pad_maximum_fusion
  259.3 0.3 copy.4
  259.6 6.0 stack.2
  265.6 5.4 all-to-all-start
  271.0 0.0 all-reduce.5.cloned.1.call-start
  271.0 283.6 %all-to-all-done = bf16[16,3,256,512]{3,2,1,0:T(8,128)(2,1)} async-done(((bf16[16,3,256,512]{3,2,1,0:T(8,128)(2,1)}), bf16[16,3,256,512]{3,2,1,0:T(8,128)(2,1)}, u32[]{:S(2)}, u32[]{:S(2)}) %all-to-all-start) | async-done | bytes 12582944 | tf_op jit(solution)/shard_map/all_to_all | solution.py:32
  554.6 1.7 select_bitcast_fusion
  556.3 0.0 all-reduce.5.cloned.1.call-update
  556.3 147.9 %all-reduce.5.cloned.1.call-done = bf16[256,512]{1,0:T(8,128)(2,1)} async-done(((bf16[256,512]{1,0:T(8,128)(2,1)}), bf16[256,512]{1,0:T(8,128)(2,1)}) %all-reduce.5.cloned.1.call-update) | async-done | bytes 262160 | tf_op jit(solution)/shard_map/psum | solution.py:9
  704.2 12.6 %subtract_convert_fusion = bf16[48,256,256]{2,1,0:T(8,128)(2,1)} fusion(bf16[48,256,256]{2,1,0:T(8,128)(2,1)} %param.5, bf16[48,256,512]{2,1,0:T(8,128)(2,1)} %bitcast.6, bf16[256,512]{1,0:T(8,128)(2,1)} %all-reduce.5.cloned.1.call-done), kind=kOutput, calls=%fused_computation | convolution fusion | flops 3230662656 | bytes 25427968 | tf_op jit(solution)/shard_map/tak,bk->tab/dot_general | solution.py:37
Async XLA Ops:
  6.5 251.0 %all-reduce.3.cloned.1.call-start = ((), (), s32[]{:S(2)}) async-start(), calls=%async_computation.1 | async-start | bytes 262144 | tf_op jit(solution)/shard_map/psum | solution.py:9
  265.6 289.0 %all-to-all-start = ((bf16[16,3,256,512]{3,2,1,0:T(8,128)(2,1)}), bf16[16,3,256,512]{3,2,1,0:T(8,128)(2,1)}, u32[]{:S(2)}, u32[]{:S(2)}) async-start(bf16[16,3,256,512]{3,2,1,0:T(8,128)(2,1)} %stack.2), calls=%async_computation | async-start | bytes 25165824 | tf_op jit(solution)/shard_map/all_to_all | solution.py:32
  271.0 433.2 %all-reduce.5.cloned.1.call-start = ((), (), s32[]{:S(2)}) async-start(), calls=%async_computation.2 | async-start | bytes 524288 | tf_op jit(solution)/shard_map/psum | solution.py:9
Sparse Core Ops, SparseCore 0:
  12.9 244.6 all-reduce.2
  556.4 147.7 all-reduce.4

commit v2 on v0

--- a/solution.py
+++ b/solution.py
@@ -6,7 +6,7 @@
 
 def broadcast(value, axis, source):
     kept = jnp.where(lax.axis_index(axis) == source, value, 0).astype(value.dtype)
-    return lax.psum(kept, axis)
+    return jnp.sum(lax.all_gather(kept, axis), axis=0)
 
 
 def shards(panel_cols, inverses, trailing):

time: 692 us -> 1140 us (1.65)
  waiting for transfers between devices: 659 us -> 1090 us
  other arithmetic: 2.4 us -> 16.1 us
    all_gather x0 -> x2, waiting for transfers between devices: none -> 824 us  [broadcast(): return jnp.sum(lax.all_gather(kept, axis), axis=0)]
    psum x2 -> x0, waiting for transfers between devices: 395 us -> none  [broadcast(): return lax.psum(kept, axis)]
    reduce_sum x0 -> x2, other arithmetic: none -> 14.3 us  [broadcast(): return jnp.sum(lax.all_gather(kept, axis), axis=0)]
where the time goes in v2:
time: 1140 us
  waiting for transfers between devices  1090 us (96%)
  other arithmetic  16.1 us (1%)
  matrix products  14.4 us (1%)
  between operations  13.2 us (1%)
    all_gather x2, waiting for transfers between devices, broadcast(): return jnp.sum(lax.all_gather(kept, axis), axis=0)  824 us
    all_gather x1, waiting for transfers between devices, shards(): whole_panel = lax.all_gather(factored, 'col', axis=0, tiled=True)  267 us
  transfers between devices with their start and end apart: 3, of which 3 were waited for; matrix products, arithmetic and copies ran while one was open for 0% of the time, Pallas kernels for 0%

profile of v2, /device:TPU:1, one launch (start us, length us, event | category | flops | bytes accessed | tf_op | source)
XLA Modules:
  0.0 1136.5 jit_solution(2214308031572921852)
XLA Ops:
  6.5 0.0 all-gather.4.cloned.1.call-start
  6.5 1.3 convolution_convert_fusion.1
  7.9 0.8 copy.5
  8.7 0.0 all-gather.4.cloned.1.call-update
  8.7 0.0 copy-start
  8.7 0.0 copy-start.1
  8.7 0.0 all-gather.6.cloned.1.call-start
  8.8 758.9 %all-gather.4.cloned.1.call-done = bf16[256,256,256]{2,1,0:T(8,128)(2,1)} async-done(((bf16[1,256,256]{2,1,0:T(8,128)(2,1)}), bf16[256,256,256]{2,1,0:T(8,128)(2,1)}) %all-gather.4.cloned.1.call-update) | async-done | bytes 33554448 | tf_op jit(solution)/shard_map/all_gather | solution.py:9
  767.6 11.5 %reduce_sum.24 = bf16[256,256]{1,0:T(8,128)(2,1)S(1)} reduce(bf16[256,256,256]{2,1,0:T(8,128)(2,1)} %all-gather.4.cloned.1.call-done, bf16[]{:T(256)} %constant.38.clone.1), dimensions={0}, to_apply=%region_0.1 | reduce | flops 16711680 | bytes 33685504 | tf_op jit(solution)/shard_map/reduce_sum | solution.py:9
  779.1 0.0 copy-done
  779.2 0.0 copy-done.1
  779.2 0.6 convolution_convert_fusion
  779.7 0.1 pad_maximum_fusion
  779.8 1.2 copy.7
  781.0 0.0 all-gather.6.cloned.1.call-update
  781.0 0.0 all-gather.8.cloned.1.call-start
  781.1 266.7 %all-gather.6.cloned.1.call-done = bf16[48,256,512]{2,1,0:T(8,128)(2,1)} async-done(((bf16[3,256,512]{2,1,0:T(8,128)(2,1)}), bf16[48,256,512]{2,1,0:T(8,128)(2,1)}) %all-gather.6.cloned.1.call-update) | async-done | bytes 12582928 | tf_op jit(solution)/shard_map/all_gather | solution.py:31
  1047.7 1.7 dynamic-slice_select_fusion
  1049.4 0.0 all-gather.8.cloned.1.call-update
  1049.4 65.1 %all-gather.8.cloned.1.call-done = bf16[16,256,512]{2,1,0:T(8,128)(2,1)} async-done(((bf16[1,256,512]{2,1,0:T(8,128)(2,1)}), bf16[16,256,512]{2,1,0:T(8,128)(2,1)}) %all-gather.8.cloned.1.call-update) | async-done | bytes 4194320 | tf_op jit(solution)/shard_map/all_gather | solution.py:9
  1114.5 2.8 reduce_sum.25
  1117.4 12.5 %subtract_convert_fusion = bf16[48,256,256]{2,1,0:T(8,128)(2,1)} fusion(bf16[48,256,256]{2,1,0:T(8,128)(2,1)} %param.5, bf16[48,256,512]{2,1,0:T(8,128)(2,1)} %all-gather.6.cloned.1.call-done, bf16[256,512]{1,0:T(8,128)(2,1)S(1)} %reduce_sum.25), kind=kOutput, calls=%fused_computation | convolution fusion | flops 3230662656 | bytes 25427968 | tf_op jit(solution)/shard_map/tak,bk->tab/dot_general | solution.py:35
  (1 shorter events, 0.0 us)
Async XLA Ops:
  6.5 761.1 %all-gather.4.cloned.1.call-start = ((), (), s32[]{:S(2)}) async-start(), calls=%async_computation | async-start | bytes 33685504 | tf_op jit(solution)/shard_map/all_gather | solution.py:9
  8.7 770.5 %copy-start = (bf16[3,256,512]{2,1,0:T(8,128)(2,1)S(1)}, bf16[3,256,512]{2,1,0:T(8,128)(2,1)}, u32[]{:S(2)}) copy-start(bf16[3,256,512]{2,1,0:T(8,128)(2,1)} %param.3) | copy-start | bytes 2359300
  8.7 770.5 %copy-start.1 = (bf16[2,256,256]{2,1,0:T(8,128)(2,1)S(1)}, bf16[2,256,256]{2,1,0:T(8,128)(2,1)}, u32[]{:S(2)}) copy-start(bf16[2,256,256]{2,1,0:T(8,128)(2,1)} %param.4) | copy-start | bytes 786436
  8.7 1039.0 %all-gather.6.cloned.1.call-start = ((), (), s32[]{:S(2)}) async-start(), calls=%async_computation.1 | async-start | bytes 13369344 | tf_op jit(solution)/shard_map/all_gather | solution.py:31
  781.0 333.5 %all-gather.8.cloned.1.call-start = ((), (), s32[]{:S(2)}) async-start(), calls=%async_computation.2 | async-start | bytes 4456448 | tf_op jit(solution)/shard_map/all_gather | solution.py:9
Sparse Core Ops, SparseCore 0:
  9.2 758.3 all-gather.3
  781.1 266.5 all-gather.5
  1050.4 64.0 all-gather.7
